TPU v7x, 32 devices: a whole 2x2x4 slice. The times are simulated.
32 devices in a mesh: mem: 8 (over z, y), lev: 4 (over x, core).
Axes of the slice: x: 2, y: 2, z: 4, core: 2. Of those that a mesh axis runs over, the one named last changes fastest.
Arguments:
- prior_ensemble_stack: float32 [16, 20, 64, 512], P('mem', 'lev'), may hold values from -6 to 6
- vertical_cfl_ratio: float32 [20, 64, 512], P('lev'), may hold values from -0.35 to 0.35
- horizontal_cfl_ratio: float32 [20, 64, 512], P('lev'), may hold values from -0.35 to 0.35
- spreading_coefficient: float32 [20], P('lev'), may hold values from 0.02 to 0.2
- obs_cells: int32 [2, 16], replicated, may hold values from 0 to 32767
- obs_slabs: int32 [2, 16], replicated, may hold values from 0 to 19
- obs_values: float32 [2, 16], replicated, may hold values from -6 to 6
- obs_error: float32 [2, 16], replicated, may hold values from 0.25 to 2
Outputs:
- analysis: float32 [16, 20, 64, 512], P('mem', 'lev')
All inputs are finite; a program needn't handle non-finite values.
Results may differ from a plain program's by a relative error of at most 0.0001.
Values sent between devices are 32-bit elements; how exact they have to be, the bound alone decides.
No kernel may reach another device: no remote copies, remote signals or barrier semaphores. Data moves between devices by JAX's collectives and lax.ppermute only.
A program may use at most 256 MiB of HBM per device.

v0:
```python
import jax
import jax.numpy as jnp
from jax import lax
from jax.sharding import PartitionSpec as P

NX = 512
STEPS = 2
LOC_HALF = 64


def predicted_model_vector(
    ensemble_gridded_values, vertical_cfl_ratio, horizontal_cfl_ratio, spreading_coefficient
):
    diffuse = spreading_coefficient[:, None, None]
    for time_step in range(STEPS):
        widths = [(0, 0)] * (ensemble_gridded_values.ndim - 2) + [(1, 1), (1, 1)]
        padded = jnp.pad(ensemble_gridded_values, widths, mode="edge")
        east_cell = padded[..., 1:-1, 2:]
        west_cell = padded[..., 1:-1, :-2]
        north_cell = padded[..., 2:, 1:-1]
        south_cell = padded[..., :-2, 1:-1]
        ensemble_gridded_values = (
            ensemble_gridded_values
            - 0.5 * vertical_cfl_ratio * (east_cell - west_cell)
            - 0.5 * horizontal_cfl_ratio * (north_cell - south_cell)
            + diffuse
            * (east_cell + west_cell + north_cell + south_cell - 4.0 * ensemble_gridded_values)
        )
    return ensemble_gridded_values


def grid_distance(cells_a, cells_b):
    row_gap = (cells_a[:, None] // NX - cells_b[None, :] // NX).astype(jnp.float32)
    col_gap = (cells_a[:, None] % NX - cells_b[None, :] % NX).astype(jnp.float32)
    return jnp.sqrt(row_gap * row_gap + col_gap * col_gap)


def gaspari_taper(dist):
    scaled = dist / LOC_HALF
    inner_portion = (
        ((-0.25 * scaled + 0.5) * scaled + 0.625) * scaled - 5.0 / 3.0
    ) * scaled * scaled + 1.0
    safe_ratio = jnp.maximum(scaled, 1.0)
    outer_portion = (
        ((((scaled / 12.0 - 0.5) * scaled + 0.625) * scaled + 5.0 / 3.0) * scaled - 5.0) * scaled
        + 4.0
        - 2.0 / (3.0 * safe_ratio)
    )
    return jnp.where(scaled <= 1.0, inner_portion, jnp.where(scaled < 2.0, outer_portion, 0.0))


def obs_space(prior_rows, row_cells, first_row, obs_cell, obs_value, obs_var):
    member_count = prior_rows.shape[1]
    reach_table = gaspari_taper(grid_distance(row_cells, obs_cell))

    def advance_obs(current, position):
        own_row = lax.dynamic_index_in_dim(current, first_row + position, 0, False)
        row_mean = jnp.mean(own_row)
        anomaly = own_row - row_mean
        spread = jnp.sum(anomaly * anomaly) / (member_count - 1) + 1e-06
        error_var = lax.dynamic_index_in_dim(obs_var, position, 0, False)
        seen_value = lax.dynamic_index_in_dim(obs_value, position, 0, False)
        shrink = jnp.sqrt(error_var / (spread + error_var))
        increment = (
            (row_mean * error_var + seen_value * spread) / (spread + error_var)
            - row_mean
            + (shrink - 1.0) * anomaly
        )
        centered = current - jnp.mean(current, axis=1, keepdims=True)
        slopes = jnp.dot(centered, anomaly, precision=lax.Precision.HIGHEST) / (
            (member_count - 1) * spread
        )
        weight = lax.dynamic_index_in_dim(reach_table, position, 1, False)
        current = current + (weight * slopes)[:, None] * increment[None, :]
        return (current, (anomaly, spread, increment))

    positions = jnp.arange(obs_cell.shape[0], dtype=jnp.int32)
    prior_rows, obs_plan = lax.scan(advance_obs, prior_rows, positions)
    return (obs_plan, prior_rows)


def settle(state_rows, obs_plan, cell_loc):
    prior_anoms, spreads, increments = obs_plan
    member_count = state_rows.shape[0]
    centered = state_rows - jnp.mean(state_rows, axis=0, keepdims=True)
    cross_cov = jnp.einsum(
        "km,msc->ksc", prior_anoms, centered, precision=lax.Precision.HIGHEST
    ) / (member_count - 1)
    incr_anom = increments - jnp.mean(increments, axis=1, keepdims=True)
    incr_link = jnp.dot(incr_anom, prior_anoms.T, precision=lax.Precision.HIGHEST) / (
        member_count - 1
    )

    def solve_step(weights, position):
        column = lax.dynamic_index_in_dim(incr_link, position, 1, False)
        summed_total = lax.dynamic_index_in_dim(cross_cov, position, 0, False) + jnp.einsum(
            "j,jsc->sc", column, weights, precision=lax.Precision.HIGHEST
        )
        taper_row = lax.dynamic_index_in_dim(cell_loc, position, 0, False)
        update_row = (
            taper_row[None, :]
            * summed_total
            / lax.dynamic_index_in_dim(spreads, position, 0, False)
        )
        return (lax.dynamic_update_index_in_dim(weights, update_row, position, 0), None)

    positions = jnp.arange(cross_cov.shape[0], dtype=jnp.int32)
    weights, unused = lax.scan(solve_step, jnp.zeros_like(cross_cov), positions)
    return state_rows + jnp.einsum(
        "km,ksc->msc", increments, weights, precision=lax.Precision.HIGHEST
    )


def pick_rows(state_rows, obs_slab, obs_cell, slab_base, cell_base):
    slab_dev = state_rows.shape[1]
    cell_dev = state_rows.shape[2]
    slab_off = obs_slab - slab_base
    cell_off = obs_cell - cell_base
    inside = (slab_off >= 0) & (slab_off < slab_dev) & (cell_off >= 0) & (cell_off < cell_dev)
    taken_rows = state_rows[
        :, jnp.clip(slab_off, 0, slab_dev - 1), jnp.clip(cell_off, 0, cell_dev - 1)
    ]
    return jnp.where(inside[:, None], taken_rows.T, 0.0)


def body(
    prior_ensemble_stack,
    vertical_cfl_ratio,
    horizontal_cfl_ratio,
    spreading_coefficient,
    obs_cells,
    obs_slabs,
    obs_values,
    obs_error,
):
    mem_dev, slab_dev, grid_rows, grid_cols = prior_ensemble_stack.shape
    cell_total = grid_rows * grid_cols
    cell_dev = cell_total // lax.axis_size("mem")
    batch_count = obs_cells.shape[0]
    ensemble_gridded_values = predicted_model_vector(
        prior_ensemble_stack, vertical_cfl_ratio, horizontal_cfl_ratio, spreading_coefficient
    )
    by_cells = ensemble_gridded_values.reshape(mem_dev, slab_dev, cell_total)
    cell_base = lax.axis_index("mem") * cell_dev
    slab_base = lax.axis_index("lev") * slab_dev
    local_cells = cell_base + jnp.arange(cell_dev, dtype=jnp.int32)
    cell_locs = [
        gaspari_taper(grid_distance(obs_cells[batch_no], local_cells))
        for batch_no in range(batch_count)
    ]
    state_rows = lax.all_to_all(by_cells, "mem", split_axis=2, concat_axis=0, tiled=True)
    for batch_no in range(batch_count):
        partial_value = pick_rows(
            state_rows, obs_slabs[batch_no], obs_cells[batch_no], slab_base, cell_base
        )
        prior_rows = lax.psum(partial_value, ("mem", "lev"))
        obs_plan, carried = obs_space(
            prior_rows,
            obs_cells[batch_no],
            0,
            obs_cells[batch_no],
            obs_values[batch_no],
            obs_error[batch_no],
        )
        state_rows = settle(state_rows, obs_plan, cell_locs[batch_no])
    result = lax.all_to_all(state_rows, "mem", split_axis=0, concat_axis=2, tiled=True)
    return result.reshape(prior_ensemble_stack.shape)


def solution(mesh):
    in_specs = (
        P("mem", "lev", None, None),
        P("lev", None, None),
        P("lev", None, None),
        P("lev"),
        P(),
        P(),
        P(),
        P(),
    )
    out_specs = P("mem", "lev", None, None)
    return jax.shard_map(body, mesh=mesh, in_specs=in_specs, out_specs=out_specs, check_vma=False)
```

profile of v0, /device:TPU:0, one launch (start us, length us, event | category | flops | bytes accessed | tf_op | source)
XLA Modules:
  0.0 932.9 jit_solution(16619717677496745712)
XLA Ops:
  1.1 1.5 broadcast_multiply_fusion.2
  2.7 2.2 multiply_add_fusion.5
  5.0 2.2 multiply_add_fusion.4
  7.2 22.3 %copy.76 = f32[2,5,64,512]{1,0,3,2:T(2,128)} copy(f32[2,5,64,512]{3,2,1,0:T(8,128)S(1)} %multiply_add_fusion.4) | data formatting | bytes 2621440 | tf_op jit(solution)/shard_map/reshape | solution.py:143
  29.5 53.2 %reshape.447 = f32[8,1,40960]{2,1,0:T(1,128)} reshape(f32[32768,2,5]{2,1,0:T(2,128)} %bitcast.261) | data formatting | bytes 2621440
  82.7 7.6 all-to-all-start
  92.0 1.6 fusion.55
  93.6 27.9 %all-to-all-done = f32[8,1,40960]{2,1,0:T(1,128)S(1)} async-done(((f32[8,1,40960]{2,1,0:T(1,128)}), f32[8,1,40960]{2,1,0:T(1,128)S(1)}, u32[]{:S(2)}, u32[]{:S(2)}) %all-to-all-start) | async-done | bytes 1310752 | tf_op jit(solution)/shard_map/all_to_all | solution.py:151
  122.0 3.8 reduce.3
  125.8 62.1 %reshape.448 = f32[32768,2,5]{2,1,0:T(2,128)} reshape(f32[8,40960]{1,0:T(8,128)S(1)} %reduce.3) | data formatting | bytes 2621440
  187.9 26.8 %copy.73 = f32[2,5,8,4096]{3,2,0,1:T(8,128)S(1)} copy(f32[2,5,8,4096]{1,0,3,2:T(2,128)} %bitcast.262) | data formatting | bytes 2621440 | tf_op jit(solution)/shard_map/all_to_all | solution.py:151
  216.8 5.5 copy.51
  222.4 1.5 gather_fusion
  223.9 37.7 %psum.14 = f32[16,16]{1,0:T(8,128)S(1)} all-reduce(f32[16,16]{1,0:T(8,128)S(1)} %broadcast_select_fusion.1), channel_id=1, replica_groups=mesh['mem'=8,'lev'=4] {'mem','lev'}, use_global_device_ids=true, to_apply=%region_0.1 | all-reduce | flops 256 | bytes 2048 | tf_op jit(solution)/shard_map/psum | solution.py:156
  261.6 153.8 %while.56 = (s32[]{:T(128)}, f32[16,16]{1,0:T(8,128)S(1)}, f32[16,16]{1,0:T(8,128)S(1)}, f32[16]{0:T(128)S(1)}, f32[16,16]{1,0:T(8,128)S(1)}, /*index=5*/s32[16]...) while((s32[]{:T(128)}, f32[16,16]{1,0:T(8,128)S(1)}, ...), condition=%wide.region_5.6_spmd, body=%wide.region_1.5_spmd.sunk | while | flops 4271 | bytes 5831 | solution.py:78
  415.9 2.2 convolution_multiply_fusion.1
  418.3 118.7 %while.57 = (s32[]{:T(128)}, f32[16,5,4096]{2,1,0:T(8,128)S(1)}, s32[16]{0:T(128)S(1)}, f32[16,4096]{1,0:T(8,128)}, f32[16,5,4096]{2,0,1:T(8,128)}, /*index=5*/f...) while((s32[]{:T(128)}, f32[16,5,4096]{2,1,0:T(8,128)S(1)}, s32[16]{0:T(128)S(1)}, ...), condition=%wide.region_9.10_spmd, body=%wide.region_8.9_spmd.sunk | while | flops 3993605 | bytes 2687667 | solution.py:108
  420.9 1.4 fusion.130
  428.3 1.4 fusion.130
  435.7 1.4 fusion.130
  443.1 1.4 fusion.130
  450.5 1.4 fusion.130
  465.4 1.4 fusion.130
  472.8 1.4 fusion.130
  480.2 1.4 fusion.130
  487.6 1.4 fusion.130
  495.1 1.4 fusion.130
  502.5 1.4 fusion.130
  509.9 1.4 fusion.130
  517.3 1.4 fusion.130
  524.7 1.4 fusion.130
  532.1 1.4 fusion.130
  537.0 3.3 fusion.97
  540.4 5.5 copy.57
  545.8 1.5 gather_fusion.1
  547.4 41.9 %psum.15 = f32[16,16]{1,0:T(8,128)S(1)} all-reduce(f32[16,16]{1,0:T(8,128)S(1)} %broadcast_select_fusion), channel_id=1, replica_groups=mesh['mem'=8,'lev'=4] {'mem','lev'}, use_global_device_ids=true, to_apply=%region_10.11 | all-reduce | flops 256 | bytes 2048 | tf_op jit(solution)/shard_map/psum | solution.py:156
  589.3 163.1 %while.58 = (s32[]{:T(128)}, f32[16,16]{1,0:T(8,128)S(1)}, f32[16,16]{1,0:T(8,128)S(1)}, f32[16]{0:T(128)S(1)}, f32[16,16]{1,0:T(8,128)S(1)}, /*index=5*/s32[16]...) while((s32[]{:T(128)}, f32[16,16]{1,0:T(8,128)S(1)}, ...), condition=%wide.region_15.16_spmd, body=%wide.region_11.15_spmd.sunk | while | flops 4271 | bytes 5831 | solution.py:78
  753.0 2.2 convolution_multiply_fusion
  755.9 120.0 %while.59 = (s32[]{:T(128)}, f32[16,5,4096]{2,1,0:T(8,128)S(1)}, s32[16]{0:T(128)S(1)}, f32[16,4096]{1,0:T(8,128)}, f32[16,5,4096]{2,0,1:T(8,128)}, /*index=5*/f...) while((s32[]{:T(128)}, f32[16,5,4096]{2,1,0:T(8,128)S(1)}, s32[16]{0:T(128)S(1)}, ...), condition=%wide.region_19.20_spmd, body=%wide.region_18.19_spmd.sunk | while | flops 3993605 | bytes 2687667 | solution.py:108
  758.5 1.4 fusion.140
  766.0 1.4 fusion.140
  773.5 1.4 fusion.140
  788.5 1.4 fusion.140
  796.0 1.4 fusion.140
  811.0 1.4 fusion.140
  818.5 1.4 fusion.140
  875.9 1.9 convolution_add_fusion
  878.6 51.7 %all_to_all.33 = f32[16,5,4096]{2,1,0:T(8,128)S(1)} all-to-all(f32[16,5,4096]{2,1,0:T(8,128)S(1)} %copy.63), channel_id=1, replica_groups=mesh['mem'=8,'lev'=4] {'mem'}, dimensions={0} | all-to-all | bytes 2621440 | tf_op jit(solution)/shard_map/all_to_all | solution.py:166
  (653 shorter events, 283.8 us)
Async XLA Ops:
  1.0 1.7 copy-start.1
  1.0 1.7 copy-start.4
  82.7 7.7 copy-start.2
  82.7 8.7 copy-start.3
  82.7 8.8 copy-start.5
  82.7 8.8 copy-start.6
  82.7 38.8 %all-to-all-start = ((f32[8,1,40960]{2,1,0:T(1,128)}), f32[8,1,40960]{2,1,0:T(1,128)S(1)}, u32[]{:S(2)}, u32[]{:S(2)}) async-start(f32[8,1,40960]{2,1,0:T(1,128)} %reshape.447), calls=%async_computation | async-start | bytes 2621440 | tf_op jit(solution)/shard_map/all_to_all | solution.py:151
  216.8 199.1 %copy-start = (f32[16,5,4096]{2,0,1:T(8,128)}, f32[16,5,4096]{2,0,1:T(8,128)S(1)}, u32[]{:S(2)}) copy-start(f32[16,5,4096]{2,0,1:T(8,128)S(1)} %all_to_all.27) | copy-start | bytes 3932164
  540.3 49.0 %copy-start.7 = (f32[16]{0:T(128)S(1)}, f32[16]{0:T(128)}, u32[]{:S(2)}) copy-start(f32[16]{0:T(128)} %get-tuple-element.825) | copy-start | bytes 196
  540.4 49.0 %copy-start.8 = (f32[16]{0:T(128)S(1)}, f32[16]{0:T(128)}, u32[]{:S(2)}) copy-start(f32[16]{0:T(128)} %get-tuple-element.824) | copy-start | bytes 196
  752.4 0.6 copy-start.9
  755.3 0.7 copy-start.10
where the time goes:
time: 946 us; the launch traced here: 933 us
  local copies, waits for them, and re-layouts  358 us (38%)
  loops' own time  250 us (26%)
  blocking collectives  131 us (14%)
  other arithmetic  83.4 us (9%)
  matrix products  73.5 us (8%)
  waiting for transfers between devices  27.9 us (3%)
    another operation x2, loops' own time, obs_space(): prior_rows, obs_plan = lax.scan(advance_obs, prior_rows, positions)  189 us
    unnamed x24, local copies, waits for them, and re-layouts  116 us
    psum x2, blocking collectives, body(): prior_rows = lax.psum(partial_value, ('mem', 'lev'))  79.6 us
    another operation x2, loops' own time, settle(): weights, unused = lax.scan(solve_step, jnp.zeros_like(cross_cov), positions)  61.9 us
    all_to_all x1, blocking collectives, body(): lax.all_to_all(state_rows, 'mem', split_axis=0, concat_axis=2, tiled=True)  51.7 us
    dot_general x32, matrix products, solve_step(): jnp.einsum('j,jsc->sc', column, weights, precision=lax.Precision.HIGHEST)  46.1 us
    dynamic_slice x64, local copies, waits for them, and re-layouts, obs_space(): prior_rows, obs_plan = lax.scan(advance_obs, prior_rows, positions)  40.3 us
    dynamic_slice x32, local copies, waits for them, and re-layouts, solve_step(): lax.dynamic_index_in_dim(cross_cov, position, 0, False)  36.9 us
  transfers between devices with their start and end apart: 1, of which 1 were waited for; matrix products, arithmetic and copies ran while one was open for 0% of the time, Pallas kernels for 0%

commit v1 on v0

--- a/solution.py
+++ b/solution.py
@@ -148,7 +148,10 @@
         gaspari_taper(grid_distance(obs_cells[batch_no], local_cells))
         for batch_no in range(batch_count)
     ]
-    state_rows = lax.all_to_all(by_cells, "mem", split_axis=2, concat_axis=0, tiled=True)
+    state_rows = jnp.concatenate(
+        lax.all_to_all(jnp.stack(jnp.split(by_cells, lax.axis_size("mem"), axis=2)), "mem", 0, 0),
+        axis=0,
+    )
     for batch_no in range(batch_count):
         partial_value = pick_rows(
             state_rows, obs_slabs[batch_no], obs_cells[batch_no], slab_base, cell_base

time: 946 us -> 764 us (0.81)
  local copies, waits for them, and re-layouts: 358 us -> 184 us
    unnamed x24 -> x29, local copies, waits for them, and re-layouts: 116 us -> 5.53 us
    all_to_all x5 -> x1, local copies, waits for them, and re-layouts: 34.7 us -> 1.14 us  [body(): lax.all_to_all(jnp.stack(jnp.split(by_cells, lax.axis_size('mem'), axis=2...]
    reshape x1, local copies, waits for them, and re-layouts: 22.3 us -> 1.11 us  [body(): by_cells = ensemble_gridded_values.reshape(mem_dev, slab_dev, cell_total)]
    dynamic_slice x32, local copies, waits for them, and re-layouts: 36.9 us -> 19.5 us  [solve_step(): lax.dynamic_index_in_dim(cross_cov, position, 0, False)]
where the time goes in v1:
time: 764 us; the launch traced here: 758 us
  loops' own time  253 us (33%)
  local copies, waits for them, and re-layouts  184 us (24%)
  blocking collectives  131 us (17%)
  other arithmetic  81 us (11%)
  matrix products  72.4 us (9%)
  waiting for transfers between devices  28.1 us (4%)
    another operation x2, loops' own time, obs_space(): prior_rows, obs_plan = lax.scan(advance_obs, prior_rows, positions)  189 us
    psum x2, blocking collectives, body(): prior_rows = lax.psum(partial_value, ('mem', 'lev'))  79.7 us
    another operation x2, loops' own time, settle(): weights, unused = lax.scan(solve_step, jnp.zeros_like(cross_cov), positions)  64.8 us
    all_to_all x1, blocking collectives, body(): lax.all_to_all(state_rows, 'mem', split_axis=0, concat_axis=2, tiled=True)  51.7 us
    dot_general x32, matrix products, solve_step(): jnp.einsum('j,jsc->sc', column, weights, precision=lax.Precision.HIGHEST)  46.1 us
    dynamic_slice x64, local copies, waits for them, and re-layouts, obs_space(): prior_rows, obs_plan = lax.scan(advance_obs, prior_rows, positions)  40.5 us
    dynamic_slice x32, local copies, waits for them, and re-layouts, solve_step(): taper_row = lax.dynamic_index_in_dim(cell_loc, position, 0, False)  29.6 us
    all_to_all x1, waiting for transfers between devices, body(): lax.all_to_all(jnp.stack(jnp.split(by_cells, lax.axis_size('mem'), axis=2...  28.1 us
  transfers between devices with their start and end apart: 1, of which 1 were waited for; matrix products, arithmetic and copies ran while one was open for 0% of the time, Pallas kernels for 0%

profile of v1, /device:TPU:0, one launch (start us, length us, event | category | flops | bytes accessed | tf_op | source)
XLA Modules:
  0.0 758.0 jit_solution(1939149092436216332)
XLA Ops:
  1.1 1.5 broadcast_multiply_fusion.2
  2.7 2.2 multiply_add_fusion.5
  5.0 2.2 multiply_add_fusion.4
  13.8 7.5 all-to-all-start
  22.9 1.6 fusion.55
  24.5 28.1 %all-to-all-done = f32[8,2,5,4096]{3,1,2,0:T(2,128)S(1)} async-done(((f32[8,2,5,4096]{3,1,2,0:T(2,128)}), f32[8,2,5,4096]{3,1,2,0:T(2,128)S(1)}, u32[]{:S(2)}, u32[]{:S(2)}) %all-to-all-start) | async-done | bytes 1310752 | tf_op jit(solution)/shard_map/all_to_all | solution.py:152
  53.8 2.2 reshape.424
  56.0 5.5 copy.39
  61.5 1.5 gather_fusion
  63.1 37.9 %psum.14 = f32[16,16]{1,0:T(8,128)S(1)} all-reduce(f32[16,16]{1,0:T(8,128)S(1)} %broadcast_select_fusion.1), channel_id=1, replica_groups=mesh['mem'=8,'lev'=4] {'mem','lev'}, use_global_device_ids=true, to_apply=%region_0.1 | all-reduce | flops 256 | bytes 2048 | tf_op jit(solution)/shard_map/psum | solution.py:159
  101.0 153.8 %while.56 = (s32[]{:T(128)}, f32[16,16]{1,0:T(8,128)S(1)}, f32[16,16]{1,0:T(8,128)S(1)}, f32[16]{0:T(128)S(1)}, f32[16,16]{1,0:T(8,128)S(1)}, /*index=5*/s32[16]...) while((s32[]{:T(128)}, f32[16,16]{1,0:T(8,128)S(1)}, ...), condition=%wide.region_5.6_spmd, body=%wide.region_1.5_spmd.sunk | while | flops 4271 | bytes 5831 | solution.py:78
  257.2 106.8 %while.57 = (s32[]{:T(128)}, f32[16,5,4096]{2,1,0:T(8,128)S(1)}, s32[16]{0:T(128)S(1)}, f32[16,4096]{1,0:T(8,128)}, f32[16,5,4096]{2,0,1:T(8,128)S(1)}, /*index=...) while((s32[]{:T(128)}, f32[16,5,4096]{2,1,0:T(8,128)S(1)}, s32[16]{0:T(128)S(1)}, ...), condition=%wide.region_9.10_spmd, body=%wide.region_8.9_spmd.sunk | while | flops 3993605 | bytes 2687667 | solution.py:108
  266.7 1.4 fusion.138
  273.3 1.4 fusion.138
  280.0 1.4 fusion.138
  286.7 1.4 fusion.138
  293.4 1.4 fusion.138
  306.7 1.4 fusion.138
  313.4 1.4 fusion.138
  320.0 1.4 fusion.138
  326.7 1.4 fusion.138
  340.1 1.4 fusion.138
  346.7 1.4 fusion.138
  353.4 1.4 fusion.138
  360.1 1.4 fusion.138
  364.0 3.3 fusion.105
  367.3 5.5 copy.45
  372.8 1.5 gather_fusion.1
  374.4 41.8 %psum.15 = f32[16,16]{1,0:T(8,128)S(1)} all-reduce(f32[16,16]{1,0:T(8,128)S(1)} %broadcast_select_fusion), channel_id=1, replica_groups=mesh['mem'=8,'lev'=4] {'mem','lev'}, use_global_device_ids=true, to_apply=%region_10.11 | all-reduce | flops 256 | bytes 2048 | tf_op jit(solution)/shard_map/psum | solution.py:159
  416.3 163.1 %while.58 = (s32[]{:T(128)}, f32[16,16]{1,0:T(8,128)S(1)}, f32[16,16]{1,0:T(8,128)S(1)}, f32[16]{0:T(128)S(1)}, f32[16,16]{1,0:T(8,128)S(1)}, /*index=5*/s32[16]...) while((s32[]{:T(128)}, f32[16,16]{1,0:T(8,128)S(1)}, ...), condition=%wide.region_15.16_spmd, body=%wide.region_11.15_spmd.sunk | while | flops 4271 | bytes 5831 | solution.py:78
  579.9 2.2 convolution_multiply_fusion
  582.8 118.7 %while.59 = (s32[]{:T(128)}, f32[16,5,4096]{2,1,0:T(8,128)S(1)}, s32[16]{0:T(128)S(1)}, f32[16,4096]{1,0:T(8,128)}, f32[16,5,4096]{2,0,1:T(8,128)}, /*index=5*/f...) while((s32[]{:T(128)}, f32[16,5,4096]{2,1,0:T(8,128)S(1)}, s32[16]{0:T(128)S(1)}, ...), condition=%wide.region_19.20_spmd, body=%wide.region_18.19_spmd.sunk | while | flops 3993605 | bytes 2687667 | solution.py:108
  585.3 1.4 fusion.148
  592.7 1.4 fusion.148
  600.2 1.4 fusion.148
  607.6 1.4 fusion.148
  622.4 1.4 fusion.148
  629.8 1.4 fusion.148
  637.3 1.4 fusion.148
  644.7 1.4 fusion.148
  652.1 1.4 fusion.148
  659.5 1.4 fusion.148
  666.9 1.4 fusion.148
  674.4 1.4 fusion.148
  681.8 1.4 fusion.148
  689.2 1.4 fusion.148
  701.5 1.9 convolution_add_fusion
  704.2 51.7 %all_to_all.20 = f32[16,5,4096]{2,1,0:T(8,128)S(1)} all-to-all(f32[16,5,4096]{2,1,0:T(8,128)S(1)} %copy.51), channel_id=1, replica_groups=mesh['mem'=8,'lev'=4] {'mem'}, dimensions={0} | all-to-all | bytes 2621440 | tf_op jit(solution)/shard_map/all_to_all | solution.py:169
  (657 shorter events, 267.5 us)
Async XLA Ops:
  1.0 1.7 copy-start.1
  1.0 1.7 copy-start.4
  13.8 7.5 copy-start.2
  13.8 8.5 %copy-start.3 = (s32[2,16]{1,0:T(2,128)S(1)}, s32[2,16]{1,0:T(2,128)}, u32[]{:S(2)}) copy-start(s32[2,16]{1,0:T(2,128)} %param.21) | copy-start | bytes 388
  13.8 8.6 %copy-start.5 = (f32[2,16]{1,0:T(2,128)S(1)}, f32[2,16]{1,0:T(2,128)}, u32[]{:S(2)}) copy-start(f32[2,16]{1,0:T(2,128)} %param.22) | copy-start | bytes 388
  13.8 8.6 %copy-start.6 = (f32[2,16]{1,0:T(2,128)S(1)}, f32[2,16]{1,0:T(2,128)}, u32[]{:S(2)}) copy-start(f32[2,16]{1,0:T(2,128)} %param.23) | copy-start | bytes 388
  13.8 38.8 %all-to-all-start = ((f32[8,2,5,4096]{3,1,2,0:T(2,128)}), f32[8,2,5,4096]{3,1,2,0:T(2,128)S(1)}, u32[]{:S(2)}, u32[]{:S(2)}) async-start(f32[8,2,5,4096]{3,1,2,0:T(2,128)} %fusion.58), calls=%async_computation | async-start | bytes 2621440 | tf_op jit(solution)/shard_map/all_to_all | solution.py:152
  56.0 199.9 %copy-start = (f32[16,5,4096]{2,0,1:T(8,128)}, f32[16,5,4096]{2,0,1:T(8,128)S(1)}, u32[]{:S(2)}) copy-start(f32[16,5,4096]{2,0,1:T(8,128)S(1)} %reshape.424) | copy-start | bytes 3932164
  367.3 48.9 %copy-start.7 = (f32[16]{0:T(128)S(1)}, f32[16]{0:T(128)}, u32[]{:S(2)}) copy-start(f32[16]{0:T(128)} %get-tuple-element.793) | copy-start | bytes 196
  367.3 48.9 %copy-start.8 = (f32[16]{0:T(128)S(1)}, f32[16]{0:T(128)}, u32[]{:S(2)}) copy-start(f32[16]{0:T(128)} %get-tuple-element.792) | copy-start | bytes 196
  579.4 0.5 copy-start.9
  582.2 0.6 copy-start.10
